TPU v7x, 32 devices: a whole 2x2x4 slice. The times are simulated.
32 devices in a mesh: tm: 4 (over z), lon: 8 (over y, x, core).
Axes of the slice: x: 2, y: 2, z: 4, core: 2. Of those that a mesh axis runs over, the one named last changes fastest.
Arguments:
- rhs_state: float32 [4, 3, 1024, 2048], P('tm', None, None, 'lon'), may hold values from -30 to 30
- innovations: float32 [4, 8192], P('tm', 'lon'), may hold values from -6 to 6
- trajectory: bfloat16 [4, 2, 3, 1024, 2048], P('tm', None, None, None, 'lon'), may hold values from -1 to 1.5, as said below
- model_var: float32 [4, 3, 1024, 2048], P('tm', None, None, 'lon'), may hold values from 0.2 to 2
- obs_var: float32 [4, 8192], P('tm', 'lon'), may hold values from 0.2 to 2
- obs_index: int32 [4, 8192], P('tm', 'lon'), may hold values from 0 to 786431, as said below
- control_rhs: float32 [4, 3, 1024, 2048], P('tm', None, None, 'lon'), may hold values from -30 to 30
Outputs:
- multiplier_out: float32 [4, 3, 1024, 2048], P('tm', None, None, 'lon')
- obs_dual_out: float32 [4, 8192], P('tm', 'lon')
- increment_out: float32 [4, 3, 1024, 2048], P('tm', None, None, 'lon')
Inputs may be any that keep to these rules, and one draw needn't show every extreme that they name: obs_index[k, j] = (field 1024 + row) * 256 + column with field 0 to 2, row 0 to 1023 and column 0 to 255 within the band j // 1024; an index may repeat. Field 0 of trajectory is the depth, fields 1 and 2 the winds.
All inputs are finite; a program needn't handle non-finite values.
Results may differ from a plain program's by a relative error of at most 0.0003.
Values sent between devices are 32-bit elements; how exact they have to be, the bound alone decides.
No kernel may reach another device: no remote copies, remote signals or barrier semaphores. Data moves between devices by JAX's collectives and lax.ppermute only.
A program may use at most 192 MiB of HBM per device.

v0:
```python
import jax
import jax.numpy as jnp
from jax import lax
from jax.sharding import PartitionSpec as P

courant = 0.25
coriolis = 0.2


def passed_along(block, axis, distance):
    devices = range(lax.axis_size(axis))
    route = [(i - distance, i) for i in devices if i - distance in devices]
    return lax.ppermute(block, axis, route)


def with_halo(shard, sides, width):
    for axis, dim in sides:
        peers, length = (lax.axis_size(axis), shard.shape[dim])
        up = [(i, (i + 1) % peers) for i in range(peers)]
        down = [(j, i) for i, j in up]
        last = lax.slice_in_dim(shard, length - width, length, axis=dim)
        first = lax.slice_in_dim(shard, 0, width, axis=dim)
        before = lax.ppermute(last, axis, up)
        after = lax.ppermute(first, axis, down)
        shard = jnp.concatenate([before, shard, after], axis=dim)
    return shard


def coriolis_rows(rows):
    position = jnp.arange(rows, dtype=jnp.float32)
    return (coriolis * ((2.0 * position + 1.0) / rows - 1.0))[:, None]


def centered_x(extended):
    return 0.5 * (extended[:, :, 2:] - extended[:, :, :-2])


def walled_y(field):
    padded = jnp.pad(field, ((0, 0), (1, 1), (0, 0)))
    return 0.5 * (padded[:, 2:, :] - padded[:, :-2, :])


def tangent_step(current, x_diffs, traj_step, rotation):
    mean_depth = traj_step[0].astype(jnp.float32)
    mean_east = traj_step[1].astype(jnp.float32)
    mean_north = traj_step[2].astype(jnp.float32)
    y_diffs = walled_y(current)
    height = current[0]
    east_wind = current[1]
    north_wind = current[2]
    new_height = height - courant * (
        mean_depth * (x_diffs[1] + y_diffs[2]) + mean_east * x_diffs[0] + mean_north * y_diffs[0]
    )
    new_east = (
        east_wind
        - courant * (x_diffs[0] + mean_east * x_diffs[1] + mean_north * y_diffs[1])
        + rotation * north_wind
    )
    new_north = (
        north_wind
        - courant * (y_diffs[0] + mean_east * x_diffs[2] + mean_north * y_diffs[2])
        - rotation * east_wind
    )
    return jnp.stack([new_height, new_east, new_north])


def east_fluxes(adjoint, traj_step):
    mean_depth = traj_step[0].astype(jnp.float32)
    mean_east = traj_step[1].astype(jnp.float32)
    return jnp.stack(
        [
            mean_east * adjoint[0] + adjoint[1],
            mean_depth * adjoint[0] + mean_east * adjoint[1],
            mean_east * adjoint[2],
        ]
    )


def north_fluxes(adjoint, traj_step):
    mean_depth = traj_step[0].astype(jnp.float32)
    mean_north = traj_step[2].astype(jnp.float32)
    return jnp.stack(
        [
            mean_north * adjoint[0] + adjoint[2],
            mean_north * adjoint[1],
            mean_depth * adjoint[0] + mean_north * adjoint[2],
        ]
    )


def adjoint_step(adjoint, x_diffs, traj_step, rotation):
    y_diffs = walled_y(north_fluxes(adjoint, traj_step))
    new_height = adjoint[0] + courant * (x_diffs[0] + y_diffs[0])
    new_east = adjoint[1] + courant * (x_diffs[1] + y_diffs[1]) - rotation * adjoint[2]
    new_north = adjoint[2] + courant * (x_diffs[2] + y_diffs[2]) + rotation * adjoint[1]
    return jnp.stack([new_height, new_east, new_north])


def apply_saddle(vector, traj_dev, model_part, obs_part, local_index, rotation):
    multiplier, obs_dual, increment = vector
    steps_total = traj_dev.shape[0]
    later = passed_along(multiplier, "tm", -1)
    current = increment
    adjoint = later
    for step_number in range(steps_total):
        extended = with_halo(current, (("lon", 2),), 1)
        current = tangent_step(current, centered_x(extended), traj_dev[step_number], rotation)
    for step_number in reversed(range(steps_total)):
        fluxes = east_fluxes(adjoint, traj_dev[step_number])
        extended = with_halo(fluxes, (("lon", 2),), 1)
        adjoint = adjoint_step(adjoint, centered_x(extended), traj_dev[step_number], rotation)
    earlier = passed_along(current, "tm", 1)
    flat_inc = increment.reshape(-1)
    observed = flat_inc[local_index]
    spread = jnp.zeros_like(flat_inc).at[local_index].add(obs_dual).reshape(increment.shape)
    row_one = model_part * multiplier + increment - earlier
    row_two = obs_part * obs_dual + observed
    row_three = multiplier - adjoint + spread
    return (row_one, row_two, row_three)


def precondition(vector, model_part, obs_part):
    return (vector[2], vector[1] / obs_part, vector[0] - model_part * vector[2])


def local_product(first_vec, second_vec):
    return (
        jnp.sum(first_vec[0] * second_vec[0])
        + jnp.sum(first_vec[1] * second_vec[1])
        + jnp.sum(first_vec[2] * second_vec[2])
    )


def scaled(vector, factor):
    return tuple((block * factor for block in vector))


def minus_scaled(vector, other, factor):
    return tuple((block - factor * piece for block, piece in zip(vector, other)))


def orthogonalize(image, basis_list):
    coef_list = []
    for vector in basis_list:
        coef_value = lax.psum(local_product(vector, image), ("tm", "lon"))
        image = minus_scaled(image, vector, coef_value)
        coef_list.append(coef_value)
    remain = lax.psum(local_product(image, image), ("tm", "lon"))
    return (image, coef_list, jnp.sqrt(remain))


def shards(rhs_state, innovations, trajectory, model_var, obs_var, obs_index, control_rhs):
    local_index = obs_index[0]
    rotation = coriolis_rows(rhs_state.shape[2])
    traj_dev = trajectory[0]
    model_part = model_var[0]
    obs_part = obs_var[0]
    start = (rhs_state[0], innovations[0], control_rhs[0])
    start_square = lax.psum(local_product(start, start), ("tm", "lon"))
    beta = jnp.sqrt(start_square)
    basis_zero = scaled(start, 1.0 / beta)
    precond_zero = precondition(basis_zero, model_part, obs_part)
    image = apply_saddle(precond_zero, traj_dev, model_part, obs_part, local_index, rotation)
    image, coef_first, below_first = orthogonalize(image, [basis_zero])
    diag_first = coef_first[0]
    basis_one = scaled(image, 1.0 / below_first)
    precond_one = precondition(basis_one, model_part, obs_part)
    image = apply_saddle(precond_one, traj_dev, model_part, obs_part, local_index, rotation)
    image, coef_second, below_second = orthogonalize(image, [basis_zero, basis_one])
    upper_second = coef_second[0]
    diag_second = coef_second[1]
    gram_zero = diag_first * diag_first + below_first * below_first
    gram_cross = diag_first * upper_second + below_first * diag_second
    gram_one = upper_second * upper_second + diag_second * diag_second + below_second * below_second
    target_zero = beta * diag_first
    target_one = beta * upper_second
    determinant = gram_zero * gram_one - gram_cross * gram_cross
    weight_zero = (gram_one * target_zero - gram_cross * target_one) / determinant
    weight_one = (gram_zero * target_one - gram_cross * target_zero) / determinant
    result = tuple(
        (
            block_a * weight_zero + block_b * weight_one
            for block_a, block_b in zip(precond_zero, precond_one)
        )
    )
    return (result[0][None], result[1][None], result[2][None])


def solution(mesh):
    in_specs = (
        P("tm", None, None, "lon"),
        P("tm", "lon"),
        P("tm", None, None, None, "lon"),
        P("tm", None, None, "lon"),
        P("tm", "lon"),
        P("tm", "lon"),
        P("tm", None, None, "lon"),
    )
    out_specs = (P("tm", None, None, "lon"), P("tm", "lon"), P("tm", None, None, "lon"))
    return jax.shard_map(shards, mesh=mesh, in_specs=in_specs, out_specs=out_specs, check_vma=False)
```

profile of v0, /device:TPU:0, one launch (start us, length us, event | category | flops | bytes accessed | tf_op | source)
XLA Modules:
  0.0 725.3 jit_solution(345166367682195843)
XLA Ops:
  2.1 3.3 multiply_reduce_fusion.9
  8.8 42.0 %psum.42 = f32[]{:T(128)} all-reduce(f32[]{:T(128)S(6)} %add.566), channel_id=1, replica_groups=mesh['tm'=4,'lon'=8] {'tm','lon'}, use_global_device_ids=true, to_apply=%region_3.0 | all-reduce | flops 1 | bytes 8 | tf_op jit(solution)/shard_map/psum | solution.py:159
  51.5 7.8 %bitcast_subtract_fusion = (f32[3,1024,256]{2,1,0:T(8,128)S(1)}, f32[3,1024,256]{2,1,0:T(8,128)}, f32[1,3,1024,256]{3,2,1,0:T(8,128)S(1)}, f32[1,3,1024,256]{3,2,1,0:T(8,128)}) fusion(f32[1,3,1024,256]{3,2,1,0:T(8,128)} %param.10, f32[1,3,1024,256]{3,2,1,0:T(8,128)} %param.7, f32[]{:T(128)S(6)} %div.60, f32[1,3,1024,256]{3,2,1,0:T(8,128)} %param.13), kind=kLoop, calls=%fused_computation.149 | loop fusion | flops 3145728 | bytes 22020100 | tf_op jit(solution)/shard_map/sub | solution.py:123
  59.3 2.4 fusion.150
  68.5 3.5 copy.55
  82.2 8.1 %subtract_multiply_fusion.4 = (f32[3,1024,256]{2,1,0:T(8,128)S(1)}, f32[3,1024,256]{2,1,0:T(8,128)S(1)}) fusion(f32[3,1024,256]{2,1,0:T(8,128)} %copy-done.19, f32[3,1024,1]{2,1,0:T(8,128)} %copy.32, f32[3,1024,1]{2,1,0:T(8,128)} %copy.30), kind=kLoop, calls=%fused_computation.171 | loop fusion | flops 4718592 | bytes 9461760 | tf_op jit(solution)/shard_map/mul | solution.py:40
  92.7 2.6 fusion.149
  97.4 2.6 collective-permute-start.7
  102.1 5.2 subtract_multiply_fusion.3
  110.7 6.5 fusion.12
  117.2 2.3 fusion.56
  119.5 20.1 %collective-permute-done = f32[3,1024,256]{2,1,0:T(8,128)} collective-permute-done((f32[3,1024,256]{2,1,0:T(8,128)}, f32[3,1024,256]{2,1,0:T(8,128)}, u32[]{:S(2)}, u32[]{:S(2)}) %collective-permute-start) | collective-permute-done | bytes 3145760 | tf_op jit(solution)/shard_map/ppermute | solution.py:13
  139.7 4.0 fusion.50
  160.5 6.8 fusion.20
  167.4 2.9 fusion.78
  171.7 2.5 fusion.45
  174.2 4.6 pad_maximum_fusion.41
  178.9 5.5 collective-permute-start.9
  184.4 12.5 %gather_fusion = f32[1024]{0:T(1024)S(1)} fusion(f32[786432]{0:T(1024)} %multiply_subtract_fusion.2, s32[1024]{0:T(1024)S(1)} %broadcast_clamp_fusion), kind=kCustom, calls=%fused_computation | custom fusion | bytes 12288 | tf_op jit(solution)/shard_map/gather | solution.py:114
  197.6 7.8 %scatter_custom_fusion = f32[786432]{0:T(1024)} fusion(s32[1024]{0:T(1024)S(1)} %bitcast.166, f32[1024]{0:T(1024)S(1)} %get-tuple-element.25, f32[]{:T(128)} %constant.11.clone.1), kind=kCustom, calls=%fused_computation.187 | custom fusion | flops 1024 | bytes 3145732 | tf_op jit(solution)/shard_map/scatter-add | solution.py:115
  205.3 4.8 reshape.519
  210.1 4.0 fusion.151
  216.0 2.4 collective-permute-start.3
  228.0 6.6 fusion.17
  238.5 3.1 pad_maximum_fusion.42
  241.6 8.9 %collective-permute-done.9 = f32[3,1024,256]{2,1,0:T(8,128)} collective-permute-done((f32[3,1024,256]{2,1,0:T(8,128)}, f32[3,1024,256]{2,1,0:T(8,128)}, u32[]{:S(2)}, u32[]{:S(2)}) %collective-permute-start.9) | collective-permute-done | bytes 3145760 | tf_op jit(solution)/shard_map/ppermute | solution.py:13
  250.5 3.6 fusion.26
  255.9 5.2 copy.56
  261.1 40.6 %psum.43 = f32[]{:T(128)} all-reduce(f32[]{:T(128)S(6)} %add.611), channel_id=1, replica_groups=mesh['tm'=4,'lon'=8] {'tm','lon'}, use_global_device_ids=true, to_apply=%region_8.9 | all-reduce | flops 1 | bytes 8 | tf_op jit(solution)/shard_map/psum | solution.py:145
  303.0 7.8 %multiply_reduce_fusion.5 = (f32[]{:T(128)}, f32[786432]{0:T(1024)}) fusion(f32[786432]{0:T(1024)} %bitcast.141, f32[]{:T(128)} %psum.43, f32[786432]{0:T(1024)} %scatter_custom_fusion, f32[786432]{0:T(1024)} %bitcast.153), kind=kLoop, calls=%fused_computation.164 | loop fusion | flops 4718591 | bytes 12582920 | tf_op jit(solution)/shard_map/reduce_sum | solution.py:130
  310.8 5.6 multiply_reduce_fusion.6
  318.4 39.2 %psum.44 = f32[]{:T(128)} all-reduce(f32[]{:T(128)S(6)} %add.614), channel_id=1, replica_groups=mesh['tm'=4,'lon'=8] {'tm','lon'}, use_global_device_ids=true, to_apply=%region_12.13 | all-reduce | flops 1 | bytes 8 | tf_op jit(solution)/shard_map/psum | solution.py:148
  358.4 9.1 %multiply_subtract_fusion.3 = (f32[3,1024,256]{2,1,0:T(8,128)S(1)}, f32[3,1024,256]{2,1,0:T(8,128)}) fusion(f32[3,1024,256]{2,1,0:T(8,128)} %get-tuple-element.23, f32[]{:T(128)S(6)} %div.64, f32[1,3,1024,256]{3,2,1,0:T(8,128)} %param.10, f32[]{:T(128)} %psum.43, f32[3,1024,256]{2,1,0:T(8,128)} %reshape.519, f32[1,1024,256]{2,1,0:T(8,128)} %copy-done.41, ...), kind=kLoop, calls=%fused_computation.176 | loop fusion | flops 7864320 | bytes 22020104 | tf_op jit(solution)/shard_map/sub | solution.py:123
  377.5 2.3 collective-permute-done.11
  381.6 8.2 %subtract_multiply_fusion.1 = (f32[3,1024,256]{2,1,0:T(8,128)S(1)}, f32[3,1024,256]{2,1,0:T(8,128)S(1)}) fusion(f32[3,1024,256]{2,1,0:T(8,128)} %copy-done, f32[3,1024,1]{2,1,0:T(8,128)} %copy.40, f32[3,1024,1]{2,1,0:T(8,128)} %copy.38), kind=kLoop, calls=%fused_computation.162 | loop fusion | flops 4718592 | bytes 9461760 | tf_op jit(solution)/shard_map/mul | solution.py:40
  392.2 2.5 fusion.147
  399.3 5.2 subtract_multiply_fusion
  407.9 6.6 fusion.8
  414.5 2.3 fusion.66
  416.8 22.2 %collective-permute-done.15 = f32[3,1024,256]{2,1,0:T(8,128)} collective-permute-done((f32[3,1024,256]{2,1,0:T(8,128)}, f32[3,1024,256]{2,1,0:T(8,128)}, u32[]{:S(2)}, u32[]{:S(2)}) %collective-permute-start.15) | collective-permute-done | bytes 3145760 | tf_op jit(solution)/shard_map/ppermute | solution.py:13
  439.0 3.9 fusion.72
  458.5 6.5 fusion.6
  465.1 4.3 fusion.100
  469.5 2.7 fusion.104
  474.4 5.3 collective-permute-start.14
  479.7 4.9 reshape.522
  486.5 5.2 copy.57
  491.7 12.5 %gather_fusion.1 = f32[1024]{0:T(1024)S(1)} fusion(f32[786432]{0:T(1024)} %bitcast.147, s32[1024]{0:T(1024)S(1)} %broadcast_clamp_fusion), kind=kCustom, calls=%fused_computation.1 | custom fusion | bytes 12288 | tf_op jit(solution)/shard_map/gather | solution.py:114
  504.8 7.8 %scatter_custom_fusion.1 = f32[786432]{0:T(1024)} fusion(s32[1024]{0:T(1024)S(1)} %bitcast.167, f32[1024]{0:T(1024)S(1)} %get-tuple-element.13, f32[]{:T(128)} %constant.11.clone.1), kind=kCustom, calls=%fused_computation.185 | custom fusion | flops 1024 | bytes 3145732 | tf_op jit(solution)/shard_map/scatter-add | solution.py:115
  512.5 4.8 reshape.521
  519.4 2.2 fusion.145
  535.2 6.7 fusion.3
  542.7 3.4 collective-permute-done.14
  546.6 6.0 pad_maximum_fusion.49
  554.4 5.2 copy.58
  559.6 40.7 %psum.45 = f32[]{:T(128)} all-reduce(f32[]{:T(128)S(6)} %add.657), channel_id=1, replica_groups=mesh['tm'=4,'lon'=8] {'tm','lon'}, use_global_device_ids=true, to_apply=%region_17.18 | all-reduce | flops 1 | bytes 8 | tf_op jit(solution)/shard_map/psum | solution.py:145
  602.8 5.5 multiply_reduce_fusion.3
  608.5 4.1 multiply_reduce_fusion.2
  615.2 39.9 %psum.46 = f32[]{:T(128)} all-reduce(f32[]{:T(128)S(6)} %add.660), channel_id=1, replica_groups=mesh['tm'=4,'lon'=8] {'tm','lon'}, use_global_device_ids=true, to_apply=%region_21.22 | all-reduce | flops 1 | bytes 8 | tf_op jit(solution)/shard_map/psum | solution.py:145
  655.8 8.1 %multiply_reduce_fusion = f32[]{:T(128)} fusion(f32[786432]{0:T(1024)} %get-tuple-element.19, f32[]{:T(128)} %psum.46, f32[]{:T(128)S(6)} %div.64, f32[786432]{0:T(1024)} %bitcast.142, f32[]{:T(128)} %psum.45, f32[786432]{0:T(1024)} %scatter_custom_fusion.1, f32[786432]{0:T(1024)} %bitcast.146), kind=kLoop, calls=%fused_computation.155 | loop fusion | flops 7077887 | bytes 12582928 | tf_op jit(solution)/shard_map/reduce_sum | solution.py:130
  666.0 2.8 multiply_reduce_fusion.1
  673.4 40.7 %psum.47 = f32[]{:T(128)} all-reduce(f32[]{:T(128)S(6)} %add.663), channel_id=1, replica_groups=mesh['tm'=4,'lon'=8] {'tm','lon'}, use_global_device_ids=true, to_apply=%region_25.26 | all-reduce | flops 1 | bytes 8 | tf_op jit(solution)/shard_map/psum | solution.py:148
  715.0 5.3 add_bitcast_fusion
  721.9 3.1 fusion.25
  (275 shorter events, 127.5 us)
Async XLA Ops:
  0.6 4.8 copy-start.54
  63.8 15.1 %collective-permute-start.5 = (f32[3,1024,1]{1,2,0:T(1,128)S(1)}, f32[3,1024,1]{1,2,0:T(1,128)S(1)}, u32[]{:S(2)}, u32[]{:S(2)}) collective-permute-start(f32[3,1024,1]{1,2,0:T(1,128)S(1)} %copy.29), channel_id=1, source_target_pairs={{1,0},{2,1},{3,2},{4,3},{5,4},{6,5},{7,6},{0,7},{9,8},{10,9},{11,1... | collective-permute-start | bytes 36872 | tf_op jit(solution)/shard_map/ppermute | solution.py:24
  66.7 13.8 %collective-permute-start.6 = (f32[3,1024,1]{1,2,0:T(1,128)S(1)}, f32[3,1024,1]{1,2,0:T(1,128)S(1)}, u32[]{:S(2)}, u32[]{:S(2)}) collective-permute-start(f32[3,1024,1]{1,2,0:T(1,128)S(1)} %copy.31), channel_id=1, source_target_pairs={{0,1},{1,2},{2,3},{3,4},{4,5},{5,6},{6,7},{7,0},{8,9},{9,10},{10,1... | collective-permute-start | bytes 36872 | tf_op jit(solution)/shard_map/ppermute | solution.py:23
  66.8 72.9 %collective-permute-start = (f32[3,1024,256]{2,1,0:T(8,128)}, f32[3,1024,256]{2,1,0:T(8,128)}, u32[]{:S(2)}, u32[]{:S(2)}) collective-permute-start(f32[3,1024,256]{2,1,0:T(8,128)} %bitcast.138), channel_id=1, source_target_pairs={{8,0},{16,8},{24,16},{9,1},{17,9},{25,17},{10,2},{18,10},{26,18},{... | collective-permute-start | bytes 9437192 | tf_op jit(solution)/shard_map/ppermute | solution.py:13
  82.2 8.1 %copy-start.6 = (bf16[1,2,3,1024,256]{4,3,2,1,0:T(8,128)(2,1)S(1)}, bf16[1,2,3,1024,256]{4,3,2,1,0:T(8,128)(2,1)}, u32[]{:S(2)}) copy-start(bf16[1,2,3,1024,256]{4,3,2,1,0:T(8,128)(2,1)} %param.9) | copy-start | bytes 9437188
  82.2 8.1 %copy-start.20 = (f32[3,1024,256]{2,1,0:T(8,128)S(1)}, f32[3,1024,256]{2,1,0:T(8,128)}, u32[]{:S(2)}) copy-start(f32[3,1024,256]{2,1,0:T(8,128)} %copy-done.19) | copy-start | bytes 9437188
  97.4 9.9 %collective-permute-start.7 = (f32[3,1024,1]{1,2,0:T(1,128)S(1)}, f32[3,1024,1]{1,2,0:T(1,128)S(1)}, u32[]{:S(2)}, u32[]{:S(2)}) collective-permute-start(f32[3,1024,1]{1,2,0:T(1,128)S(1)} %copy.33), channel_id=1, source_target_pairs={{1,0},{2,1},{3,2},{4,3},{5,4},{6,5},{7,6},{0,7},{9,8},{10,9},{11,1... | collective-permute-start | bytes 36872 | tf_op jit(solution)/shard_map/ppermute | solution.py:24
  101.9 7.1 collective-permute-start.8
  110.7 6.5 copy-start.7
  110.7 6.5 copy-start.27
  110.7 6.5 copy-start.46
  110.7 6.5 copy-start.48
  149.3 7.8 %collective-permute-start.1 = (f32[3,1024,1]{1,2,0:T(1,128)S(1)}, f32[3,1024,1]{1,2,0:T(1,128)S(1)}, u32[]{:S(2)}, u32[]{:S(2)}) collective-permute-start(f32[3,1024,1]{1,2,0:T(1,128)S(1)} %copy.21), channel_id=1, source_target_pairs={{1,0},{2,1},{3,2},{4,3},{5,4},{6,5},{7,6},{0,7},{9,8},{10,9},{11,1... | collective-permute-start | bytes 36872 | tf_op jit(solution)/shard_map/ppermute | solution.py:24
  152.9 5.9 collective-permute-start.2
  160.5 6.8 copy-start.8
  160.5 6.8 copy-start.56
  174.2 4.7 copy-start.74
  174.2 10.1 %copy-start.86 = (s32[1,1024]{1,0:T(1,128)S(1)}, s32[1,1024]{1,0:T(1,128)}, u32[]{:S(2)}) copy-start(s32[1,1024]{1,0:T(1,128)} %param.12) | copy-start | bytes 12292
  178.9 18.0 %copy-start.85 = (f32[1,1024]{1,0:T(1,128)S(1)}, f32[1,1024]{1,0:T(1,128)}, u32[]{:S(2)}) copy-start(f32[1,1024]{1,0:T(1,128)} %param.8) | copy-start | bytes 12292
  178.9 18.1 %copy-start.84 = (f32[1,1024]{1,0:T(1,128)S(1)}, f32[1,1024]{1,0:T(1,128)}, u32[]{:S(2)}) copy-start(f32[1,1024]{1,0:T(1,128)} %param.11) | copy-start | bytes 12292
  178.9 71.6 %collective-permute-start.9 = (f32[3,1024,256]{2,1,0:T(8,128)}, f32[3,1024,256]{2,1,0:T(8,128)}, u32[]{:S(2)}, u32[]{:S(2)}) collective-permute-start(f32[3,1024,256]{2,1,0:T(8,128)} %get-tuple-element.105), channel_id=1, source_target_pairs={{0,8},{8,16},{16,24},{1,9},{9,17},{17,25},{2,10},{10,18},{18,26},{... | collective-permute-start | bytes 9437192 | tf_op jit(solution)/shard_map/ppermute | solution.py:13
  216.0 8.5 %collective-permute-start.3 = (f32[3,1024,1]{1,2,0:T(1,128)S(1)}, f32[3,1024,1]{1,2,0:T(1,128)S(1)}, u32[]{:S(2)}, u32[]{:S(2)}) collective-permute-start(f32[3,1024,1]{1,2,0:T(1,128)S(1)} %copy.25), channel_id=1, source_target_pairs={{1,0},{2,1},{3,2},{4,3},{5,4},{6,5},{7,6},{0,7},{9,8},{10,9},{11,1... | collective-permute-start | bytes 36872 | tf_op jit(solution)/shard_map/ppermute | solution.py:24
  220.3 6.0 collective-permute-start.4
  227.9 6.6 copy-start.57
  227.9 6.6 copy-start.67
  227.9 6.6 copy-start.69
  227.9 6.6 copy-start.71
  235.2 6.4 copy-start.39
  235.2 6.4 copy-start.41
  235.2 6.4 copy-start.43
  238.5 11.9 %copy-start.16 = (f32[3,1024,256]{2,1,0:T(8,128)S(1)}, f32[3,1024,256]{2,1,0:T(8,128)}, u32[]{:S(2)}) copy-start(f32[3,1024,256]{2,1,0:T(8,128)} %get-tuple-element.27) | copy-start | bytes 9437188
  303.0 7.8 %copy-start.17 = (f32[3,1024,256]{2,1,0:T(8,128)S(1)}, f32[3,1024,256]{2,1,0:T(8,128)}, u32[]{:S(2)}) copy-start(f32[3,1024,256]{2,1,0:T(8,128)} %get-tuple-element.27) | copy-start | bytes 9437188
  367.5 71.4 %collective-permute-start.15 = (f32[3,1024,256]{2,1,0:T(8,128)}, f32[3,1024,256]{2,1,0:T(8,128)}, u32[]{:S(2)}, u32[]{:S(2)}) collective-permute-start(f32[3,1024,256]{2,1,0:T(8,128)} %get-tuple-element.17), channel_id=1, source_target_pairs={{8,0},{16,8},{24,16},{9,1},{17,9},{25,17},{10,2},{18,10},{26,18},{... | collective-permute-start | bytes 9437192 | tf_op jit(solution)/shard_map/ppermute | solution.py:13
  372.8 3.0 collective-permute-start.10
  375.8 4.0 collective-permute-start.11
  381.5 8.2 %copy-start.1 = (f32[3,1024,256]{2,1,0:T(8,128)S(1)}, f32[3,1024,256]{2,1,0:T(8,128)}, u32[]{:S(2)}) copy-start(f32[3,1024,256]{2,1,0:T(8,128)} %copy-done) | copy-start | bytes 9437188
  381.5 8.2 %copy-start.9 = (bf16[1,2,3,1024,256]{4,3,2,1,0:T(8,128)(2,1)S(1)}, bf16[1,2,3,1024,256]{4,3,2,1,0:T(8,128)(2,1)}, u32[]{:S(2)}) copy-start(bf16[1,2,3,1024,256]{4,3,2,1,0:T(8,128)(2,1)} %param.9) | copy-start | bytes 9437188
  396.7 7.8 %collective-permute-start.12 = (f32[3,1024,1]{1,2,0:T(1,128)S(1)}, f32[3,1024,1]{1,2,0:T(1,128)S(1)}, u32[]{:S(2)}, u32[]{:S(2)}) collective-permute-start(f32[3,1024,1]{1,2,0:T(1,128)S(1)} %copy.41), channel_id=1, source_target_pairs={{1,0},{2,1},{3,2},{4,3},{5,4},{6,5},{7,6},{0,7},{9,8},{10,9},{11,1... | collective-permute-start | bytes 36872 | tf_op jit(solution)/shard_map/ppermute | solution.py:24
  398.9 7.3 %collective-permute-start.13 = (f32[3,1024,1]{1,2,0:T(1,128)S(1)}, f32[3,1024,1]{1,2,0:T(1,128)S(1)}, u32[]{:S(2)}, u32[]{:S(2)}) collective-permute-start(f32[3,1024,1]{1,2,0:T(1,128)S(1)} %copy.43), channel_id=1, source_target_pairs={{0,1},{1,2},{2,3},{3,4},{4,5},{5,6},{6,7},{7,0},{8,9},{9,10},{10,1... | collective-permute-start | bytes 36872 | tf_op jit(solution)/shard_map/ppermute | solution.py:23
  407.9 6.6 copy-start.10
  407.9 6.6 copy-start.29
  407.9 6.6 copy-start.50
  407.9 6.6 copy-start.52
  448.5 6.7 collective-permute-start.16
  450.5 6.4 collective-permute-start.17
  458.5 6.6 copy-start.11
  458.5 6.6 copy-start.58
  474.4 71.7 %collective-permute-start.14 = (f32[3,1024,256]{2,1,0:T(8,128)}, f32[3,1024,256]{2,1,0:T(8,128)}, u32[]{:S(2)}, u32[]{:S(2)}) collective-permute-start(f32[3,1024,256]{2,1,0:T(8,128)} %pad_maximum_fusion.46), channel_id=1, source_target_pairs={{0,8},{8,16},{16,24},{1,9},{9,17},{17,25},{2,10},{10,18},{18,26},{... | collective-permute-start | bytes 9437192 | tf_op jit(solution)/shard_map/ppermute | solution.py:13
  523.5 8.3 %collective-permute-start.18 = (f32[3,1024,1]{1,2,0:T(1,128)S(1)}, f32[3,1024,1]{1,2,0:T(1,128)S(1)}, u32[]{:S(2)}, u32[]{:S(2)}) collective-permute-start(f32[3,1024,1]{1,2,0:T(1,128)S(1)} %copy.49), channel_id=1, source_target_pairs={{1,0},{2,1},{3,2},{4,3},{5,4},{6,5},{7,6},{0,7},{9,8},{10,9},{11,1... | collective-permute-start | bytes 36872 | tf_op jit(solution)/shard_map/ppermute | solution.py:24
  527.3 6.2 collective-permute-start.19
  535.1 6.7 copy-start.55
  535.2 6.7 copy-start.61
  535.2 6.7 copy-start.63
  535.2 6.7 copy-start.65
  602.8 5.5 copy-start.13
  602.8 5.5 copy-start.21
  602.8 5.6 copy-start.25
  655.8 10.2 %copy-start.18 = (f32[3,1024,256]{2,1,0:T(8,128)S(1)}, f32[3,1024,256]{2,1,0:T(8,128)}, u32[]{:S(2)}) copy-start(f32[3,1024,256]{2,1,0:T(8,128)} %get-tuple-element.23) | copy-start | bytes 9437188
  655.8 10.2 %copy-start.22 = (f32[3,1024,256]{2,1,0:T(8,128)S(1)}, f32[3,1024,256]{2,1,0:T(8,128)}, u32[]{:S(2)}) copy-start(f32[3,1024,256]{2,1,0:T(8,128)} %get-tuple-element.74) | copy-start | bytes 9437188
  714.9 7.0 copy-start.5
  714.9 7.0 copy-start.40
  714.9 7.0 copy-start.42
  715.0 7.0 copy-start.44
  715.0 7.0 copy-start.59
  (43 other events, 123.2 us)
where the time goes:
time: 731 us; the launch traced here: 725 us
  blocking collectives  243 us (33%)
  other arithmetic  224 us (31%)
  local copies, waits for them, and re-layouts  152 us (21%)
  waiting for transfers between devices  56.9 us (8%)
  starting transfers between devices  26.4 us (4%)
  between operations  22.8 us (3%)
    psum x3, blocking collectives, orthogonalize(): coef_value = lax.psum(local_product(vector, image), ('tm', 'lon'))  121 us
    psum x2, blocking collectives, orthogonalize(): remain = lax.psum(local_product(image, image), ('tm', 'lon'))  80 us
    ppermute x4, waiting for transfers between devices, passed_along(): return lax.ppermute(block, axis, route)  54.5 us
    psum x1, blocking collectives, shards(): start_square = lax.psum(local_product(start, start), ('tm', 'lon'))  42 us
    mul x6, other arithmetic, centered_x(): return 0.5 * (extended[:, :, 2:] - extended[:, :, :-2])  39.7 us
    slice x16, local copies, waits for them, and re-layouts, with_halo(): first = lax.slice_in_dim(shard, 0, width, axis=dim)  35.3 us
    unnamed x180, local copies, waits for them, and re-layouts  35.2 us
    mul x8, other arithmetic, walled_y(): return 0.5 * (padded[:, 2:, :] - padded[:, :-2, :])  35 us
  transfers between devices with their start and end apart: 20, of which 5 were waited for; matrix products, arithmetic and copies ran while one was open for 30% of the time, Pallas kernels for 0%

commit v1 on v0

--- a/solution.py
+++ b/solution.py
@@ -142,7 +142,7 @@
 def orthogonalize(image, basis_list):
     coef_list = []
     for vector in basis_list:
-        coef_value = lax.psum(local_product(vector, image), ("tm", "lon"))
+        coef_value = lax.psum(lax.psum(local_product(vector, image), "lon"), "tm")
         image = minus_scaled(image, vector, coef_value)
         coef_list.append(coef_value)
     remain = lax.psum(local_product(image, image), ("tm", "lon"))

time: 731 us -> 680 us (0.930)
  blocking collectives: 243 us -> 191 us
    psum x3 -> x6, blocking collectives: 121 us -> 72.6 us  [orthogonalize(): coef_value = lax.psum(lax.psum(local_product(vector, image), 'lon'), 'tm')]
  transfers between devices with their start and end apart: 20 -> 20, of which waited for: 5 -> 5; matrix products, arithmetic and copies ran while one was open for 30% -> 32% of each run, Pallas kernels for 0% -> 0%
where the time goes in v1:
time: 680 us; the launch traced here: 674 us
  other arithmetic  224 us (33%)
  blocking collectives  191 us (28%)
  local copies, waits for them, and re-layouts  152 us (22%)
  waiting for transfers between devices  56.9 us (8%)
  starting transfers between devices  26.6 us (4%)
  between operations  23 us (3%)
    psum x2, blocking collectives, orthogonalize(): remain = lax.psum(local_product(image, image), ('tm', 'lon'))  76.9 us
    psum x6, blocking collectives, orthogonalize(): coef_value = lax.psum(lax.psum(local_product(vector, image), 'lon'), 'tm')  72.6 us
    ppermute x4, waiting for transfers between devices, passed_along(): return lax.ppermute(block, axis, route)  54.5 us
    psum x1, blocking collectives, shards(): start_square = lax.psum(local_product(start, start), ('tm', 'lon'))  42 us
    mul x6, other arithmetic, centered_x(): return 0.5 * (extended[:, :, 2:] - extended[:, :, :-2])  39.9 us
    slice x16, local copies, waits for them, and re-layouts, with_halo(): first = lax.slice_in_dim(shard, 0, width, axis=dim)  35.3 us
    unnamed x180, local copies, waits for them, and re-layouts  35.1 us
    mul x8, other arithmetic, walled_y(): return 0.5 * (padded[:, 2:, :] - padded[:, :-2, :])  34.9 us
  transfers between devices with their start and end apart: 20, of which 5 were waited for; matrix products, arithmetic and copies ran while one was open for 32% of the time, Pallas kernels for 0%

profile of v1, /device:TPU:0, one launch (start us, length us, event | category | flops | bytes accessed | tf_op | source)
XLA Modules:
  0.0 673.9 jit_solution(10916087388234075831)
XLA Ops:
  2.1 3.3 multiply_reduce_fusion.9
  8.8 42.0 %psum.63 = f32[]{:T(128)} all-reduce(f32[]{:T(128)S(6)} %add.572), channel_id=1, replica_groups=mesh['tm'=4,'lon'=8] {'tm','lon'}, use_global_device_ids=true, to_apply=%region_3.0 | all-reduce | flops 1 | bytes 8 | tf_op jit(solution)/shard_map/psum | solution.py:159
  51.5 7.8 %bitcast_subtract_fusion = (f32[3,1024,256]{2,1,0:T(8,128)S(1)}, f32[3,1024,256]{2,1,0:T(8,128)}, f32[1,3,1024,256]{3,2,1,0:T(8,128)S(1)}, f32[1,3,1024,256]{3,2,1,0:T(8,128)}) fusion(f32[1,3,1024,256]{3,2,1,0:T(8,128)} %param.10, f32[1,3,1024,256]{3,2,1,0:T(8,128)} %param.7, f32[]{:T(128)S(6)} %div.60, f32[1,3,1024,256]{3,2,1,0:T(8,128)} %param.13), kind=kLoop, calls=%fused_computation.149 | loop fusion | flops 3145728 | bytes 22020100 | tf_op jit(solution)/shard_map/sub | solution.py:123
  59.3 2.4 fusion.150
  68.4 3.5 copy.55
  82.1 8.0 %subtract_multiply_fusion.4 = (f32[3,1024,256]{2,1,0:T(8,128)S(1)}, f32[3,1024,256]{2,1,0:T(8,128)S(1)}) fusion(f32[3,1024,256]{2,1,0:T(8,128)} %copy-done.19, f32[3,1024,1]{2,1,0:T(8,128)} %copy.32, f32[3,1024,1]{2,1,0:T(8,128)} %copy.30), kind=kLoop, calls=%fused_computation.171 | loop fusion | flops 4718592 | bytes 9461760 | tf_op jit(solution)/shard_map/mul | solution.py:40
  92.5 2.7 fusion.149
  97.2 2.6 collective-permute-start.7
  102.3 5.2 subtract_multiply_fusion.3
  110.8 6.5 fusion.12
  119.7 20.0 %collective-permute-done = f32[3,1024,256]{2,1,0:T(8,128)} collective-permute-done((f32[3,1024,256]{2,1,0:T(8,128)}, f32[3,1024,256]{2,1,0:T(8,128)}, u32[]{:S(2)}, u32[]{:S(2)}) %collective-permute-start) | collective-permute-done | bytes 3145760 | tf_op jit(solution)/shard_map/ppermute | solution.py:13
  139.7 3.9 fusion.50
  160.4 6.8 %fusion.20 = f32[3,1024,256]{2,1,0:T(8,128)S(1)} fusion(f32[3,1024,1]{2,1,0:T(8,128)} %copy.24, f32[1,1024,256]{2,1,0:T(8,128)} %copy-done.76, f32[1,1024,256]{2,1,0:T(8,128)} %copy-done.77, f32[1,1024,256]{2,1,0:T(8,128)} %copy-done.75, f32[3,1024,1]{2,1,0:T(8,128)} %copy.22), kind=kLoop, calls=%fused_computation.121 | loop fusion | flops 6291456 | bytes 6316032 | tf_op jit(solution)/shard_map/mul | solution.py:35
  167.3 2.9 fusion.78
  171.6 2.4 fusion.45
  174.1 4.6 pad_maximum_fusion.41
  178.8 5.4 collective-permute-start.9
  184.3 12.5 %gather_fusion = f32[1024]{0:T(1024)S(1)} fusion(f32[786432]{0:T(1024)} %multiply_subtract_fusion.2, s32[1024]{0:T(1024)S(1)} %broadcast_clamp_fusion), kind=kCustom, calls=%fused_computation | custom fusion | bytes 12288 | tf_op jit(solution)/shard_map/gather | solution.py:114
  197.4 7.8 %scatter_custom_fusion = f32[786432]{0:T(1024)} fusion(s32[1024]{0:T(1024)S(1)} %bitcast.166, f32[1024]{0:T(1024)S(1)} %get-tuple-element.25, f32[]{:T(128)} %constant.11.clone.1), kind=kCustom, calls=%fused_computation.187 | custom fusion | flops 1024 | bytes 3145732 | tf_op jit(solution)/shard_map/scatter-add | solution.py:115
  205.2 4.8 reshape.519
  210.0 4.0 fusion.151
  215.9 2.4 collective-permute-start.3
  227.8 6.6 fusion.17
  238.4 3.1 pad_maximum_fusion.42
  241.5 8.9 %collective-permute-done.9 = f32[3,1024,256]{2,1,0:T(8,128)} collective-permute-done((f32[3,1024,256]{2,1,0:T(8,128)}, f32[3,1024,256]{2,1,0:T(8,128)}, u32[]{:S(2)}, u32[]{:S(2)}) %collective-permute-start.9) | collective-permute-done | bytes 3145760 | tf_op jit(solution)/shard_map/ppermute | solution.py:13
  250.4 3.6 fusion.26
  256.0 13.5 %psum.64 = f32[]{:T(128)} all-reduce(f32[]{:T(128)S(6)} %add.617), channel_id=1, replica_groups=mesh['tm'=4,'lon'=8] {'lon'}, use_global_device_ids=true, to_apply=%region_8.9 | all-reduce | flops 1 | bytes 8 | tf_op jit(solution)/shard_map/psum | solution.py:145
  269.5 5.2 copy.56
  274.7 11.7 %psum.65 = f32[]{:T(128)} all-reduce(f32[]{:T(128)} %psum.64), channel_id=1, replica_groups=mesh['tm'=4,'lon'=8] {'tm'}, use_global_device_ids=true, to_apply=%region_9.10 | all-reduce | flops 1 | bytes 8 | tf_op jit(solution)/shard_map/psum | solution.py:145
  287.8 7.8 %multiply_reduce_fusion.5 = (f32[]{:T(128)}, f32[786432]{0:T(1024)}) fusion(f32[786432]{0:T(1024)} %bitcast.141, f32[]{:T(128)} %psum.65, f32[786432]{0:T(1024)} %scatter_custom_fusion, f32[786432]{0:T(1024)} %bitcast.153), kind=kLoop, calls=%fused_computation.164 | loop fusion | flops 4718591 | bytes 12582920 | tf_op jit(solution)/shard_map/reduce_sum | solution.py:130
  295.5 5.7 multiply_reduce_fusion.6
  303.2 37.9 %psum.66 = f32[]{:T(128)} all-reduce(f32[]{:T(128)S(6)} %add.620), channel_id=1, replica_groups=mesh['tm'=4,'lon'=8] {'tm','lon'}, use_global_device_ids=true, to_apply=%region_13.14 | all-reduce | flops 1 | bytes 8 | tf_op jit(solution)/shard_map/psum | solution.py:148
  341.8 9.2 %multiply_subtract_fusion.3 = (f32[3,1024,256]{2,1,0:T(8,128)S(1)}, f32[3,1024,256]{2,1,0:T(8,128)}) fusion(f32[3,1024,256]{2,1,0:T(8,128)} %get-tuple-element.23, f32[]{:T(128)S(6)} %div.64, f32[1,3,1024,256]{3,2,1,0:T(8,128)} %param.10, f32[]{:T(128)} %psum.65, f32[3,1024,256]{2,1,0:T(8,128)} %reshape.519, f32[1,1024,256]{2,1,0:T(8,128)} %copy-done.41, ...), kind=kLoop, calls=%fused_computation.176 | loop fusion | flops 7864320 | bytes 22020104 | tf_op jit(solution)/shard_map/sub | solution.py:123
  360.9 2.3 collective-permute-done.11
  364.9 8.1 %subtract_multiply_fusion.1 = (f32[3,1024,256]{2,1,0:T(8,128)S(1)}, f32[3,1024,256]{2,1,0:T(8,128)S(1)}) fusion(f32[3,1024,256]{2,1,0:T(8,128)} %copy-done, f32[3,1024,1]{2,1,0:T(8,128)} %copy.40, f32[3,1024,1]{2,1,0:T(8,128)} %copy.38), kind=kLoop, calls=%fused_computation.162 | loop fusion | flops 4718592 | bytes 9461760 | tf_op jit(solution)/shard_map/mul | solution.py:40
  375.5 2.5 fusion.147
  382.8 5.2 subtract_multiply_fusion
  391.4 6.7 fusion.8
  400.4 22.2 %collective-permute-done.15 = f32[3,1024,256]{2,1,0:T(8,128)} collective-permute-done((f32[3,1024,256]{2,1,0:T(8,128)}, f32[3,1024,256]{2,1,0:T(8,128)}, u32[]{:S(2)}, u32[]{:S(2)}) %collective-permute-start.15) | collective-permute-done | bytes 3145760 | tf_op jit(solution)/shard_map/ppermute | solution.py:13
  422.5 3.9 fusion.72
  442.0 6.7 fusion.6
  448.8 4.2 fusion.100
  453.2 2.8 fusion.104
  458.1 5.4 collective-permute-start.14
  463.5 4.9 reshape.522
  470.5 5.2 copy.57
  475.7 12.5 %gather_fusion.1 = f32[1024]{0:T(1024)S(1)} fusion(f32[786432]{0:T(1024)} %bitcast.147, s32[1024]{0:T(1024)S(1)} %broadcast_clamp_fusion), kind=kCustom, calls=%fused_computation.1 | custom fusion | bytes 12288 | tf_op jit(solution)/shard_map/gather | solution.py:114
  488.8 7.8 %scatter_custom_fusion.1 = f32[786432]{0:T(1024)} fusion(s32[1024]{0:T(1024)S(1)} %bitcast.167, f32[1024]{0:T(1024)S(1)} %get-tuple-element.13, f32[]{:T(128)} %constant.11.clone.1), kind=kCustom, calls=%fused_computation.185 | custom fusion | flops 1024 | bytes 3145732 | tf_op jit(solution)/shard_map/scatter-add | solution.py:115
  496.6 4.8 reshape.521
  519.0 6.6 fusion.3
  526.4 3.5 collective-permute-done.14
  530.3 6.0 pad_maximum_fusion.49
  538.3 15.1 %psum.67 = f32[]{:T(128)} all-reduce(f32[]{:T(128)S(6)} %add.663), channel_id=1, replica_groups=mesh['tm'=4,'lon'=8] {'lon'}, use_global_device_ids=true, to_apply=%region_18.19 | all-reduce | flops 1 | bytes 8 | tf_op jit(solution)/shard_map/psum | solution.py:145
  553.4 5.2 copy.58
  558.6 9.9 %psum.68 = f32[]{:T(128)} all-reduce(f32[]{:T(128)} %psum.67), channel_id=1, replica_groups=mesh['tm'=4,'lon'=8] {'tm'}, use_global_device_ids=true, to_apply=%region_19.20 | all-reduce | flops 1 | bytes 8 | tf_op jit(solution)/shard_map/psum | solution.py:145
  569.9 5.5 multiply_reduce_fusion.3
  575.5 4.1 multiply_reduce_fusion.2
  582.8 12.3 %psum.69 = f32[]{:T(128)} all-reduce(f32[]{:T(128)S(6)} %add.666), channel_id=1, replica_groups=mesh['tm'=4,'lon'=8] {'lon'}, use_global_device_ids=true, to_apply=%region_23.24 | all-reduce | flops 1 | bytes 8 | tf_op jit(solution)/shard_map/psum | solution.py:145
  595.8 10.0 %psum.70 = f32[]{:T(128)} all-reduce(f32[]{:T(128)} %psum.69), channel_id=1, replica_groups=mesh['tm'=4,'lon'=8] {'tm'}, use_global_device_ids=true, to_apply=%region_24.25 | all-reduce | flops 1 | bytes 8 | tf_op jit(solution)/shard_map/psum | solution.py:145
  606.4 8.1 %multiply_reduce_fusion = f32[]{:T(128)} fusion(f32[786432]{0:T(1024)} %get-tuple-element.19, f32[]{:T(128)} %psum.70, f32[]{:T(128)S(6)} %div.64, f32[786432]{0:T(1024)} %bitcast.142, f32[]{:T(128)} %psum.68, f32[786432]{0:T(1024)} %scatter_custom_fusion.1, f32[786432]{0:T(1024)} %bitcast.146), kind=kLoop, calls=%fused_computation.155 | loop fusion | flops 7077887 | bytes 12582928 | tf_op jit(solution)/shard_map/reduce_sum | solution.py:130
  616.4 2.8 multiply_reduce_fusion.1
  623.6 39.0 %psum.71 = f32[]{:T(128)} all-reduce(f32[]{:T(128)S(6)} %add.669), channel_id=1, replica_groups=mesh['tm'=4,'lon'=8] {'tm','lon'}, use_global_device_ids=true, to_apply=%region_28.29 | all-reduce | flops 1 | bytes 8 | tf_op jit(solution)/shard_map/psum | solution.py:148
  663.5 5.3 add_bitcast_fusion
  670.5 3.2 fusion.25
  (278 shorter events, 134.2 us)
Async XLA Ops:
  0.6 4.8 copy-start.54
  63.8 14.9 %collective-permute-start.5 = (f32[3,1024,1]{1,2,0:T(1,128)S(1)}, f32[3,1024,1]{1,2,0:T(1,128)S(1)}, u32[]{:S(2)}, u32[]{:S(2)}) collective-permute-start(f32[3,1024,1]{1,2,0:T(1,128)S(1)} %copy.29), channel_id=1, source_target_pairs={{1,0},{2,1},{3,2},{4,3},{5,4},{6,5},{7,6},{0,7},{9,8},{10,9},{11,1... | collective-permute-start | bytes 36872 | tf_op jit(solution)/shard_map/ppermute | solution.py:24
  66.8 13.6 %collective-permute-start.6 = (f32[3,1024,1]{1,2,0:T(1,128)S(1)}, f32[3,1024,1]{1,2,0:T(1,128)S(1)}, u32[]{:S(2)}, u32[]{:S(2)}) collective-permute-start(f32[3,1024,1]{1,2,0:T(1,128)S(1)} %copy.31), channel_id=1, source_target_pairs={{0,1},{1,2},{2,3},{3,4},{4,5},{5,6},{6,7},{7,0},{8,9},{9,10},{10,1... | collective-permute-start | bytes 36872 | tf_op jit(solution)/shard_map/ppermute | solution.py:23
  66.8 72.9 %collective-permute-start = (f32[3,1024,256]{2,1,0:T(8,128)}, f32[3,1024,256]{2,1,0:T(8,128)}, u32[]{:S(2)}, u32[]{:S(2)}) collective-permute-start(f32[3,1024,256]{2,1,0:T(8,128)} %bitcast.138), channel_id=1, source_target_pairs={{8,0},{16,8},{24,16},{9,1},{17,9},{25,17},{10,2},{18,10},{26,18},{... | collective-permute-start | bytes 9437192 | tf_op jit(solution)/shard_map/ppermute | solution.py:13
  82.1 8.0 %copy-start.6 = (bf16[1,2,3,1024,256]{4,3,2,1,0:T(8,128)(2,1)S(1)}, bf16[1,2,3,1024,256]{4,3,2,1,0:T(8,128)(2,1)}, u32[]{:S(2)}) copy-start(bf16[1,2,3,1024,256]{4,3,2,1,0:T(8,128)(2,1)} %param.9) | copy-start | bytes 9437188
  82.1 8.0 %copy-start.20 = (f32[3,1024,256]{2,1,0:T(8,128)S(1)}, f32[3,1024,256]{2,1,0:T(8,128)}, u32[]{:S(2)}) copy-start(f32[3,1024,256]{2,1,0:T(8,128)} %copy-done.19) | copy-start | bytes 9437188
  97.2 10.3 %collective-permute-start.7 = (f32[3,1024,1]{1,2,0:T(1,128)S(1)}, f32[3,1024,1]{1,2,0:T(1,128)S(1)}, u32[]{:S(2)}, u32[]{:S(2)}) collective-permute-start(f32[3,1024,1]{1,2,0:T(1,128)S(1)} %copy.33), channel_id=1, source_target_pairs={{1,0},{2,1},{3,2},{4,3},{5,4},{6,5},{7,6},{0,7},{9,8},{10,9},{11,1... | collective-permute-start | bytes 36872 | tf_op jit(solution)/shard_map/ppermute | solution.py:24
  101.7 7.4 %collective-permute-start.8 = (f32[3,1024,1]{1,2,0:T(1,128)S(1)}, f32[3,1024,1]{1,2,0:T(1,128)S(1)}, u32[]{:S(2)}, u32[]{:S(2)}) collective-permute-start(f32[3,1024,1]{1,2,0:T(1,128)S(1)} %copy.35), channel_id=1, source_target_pairs={{0,1},{1,2},{2,3},{3,4},{4,5},{5,6},{6,7},{7,0},{8,9},{9,10},{10,1... | collective-permute-start | bytes 36872 | tf_op jit(solution)/shard_map/ppermute | solution.py:23
  110.8 6.5 copy-start.7
  110.8 6.5 copy-start.27
  110.8 6.5 copy-start.46
  110.8 6.6 copy-start.48
  149.3 7.8 %collective-permute-start.1 = (f32[3,1024,1]{1,2,0:T(1,128)S(1)}, f32[3,1024,1]{1,2,0:T(1,128)S(1)}, u32[]{:S(2)}, u32[]{:S(2)}) collective-permute-start(f32[3,1024,1]{1,2,0:T(1,128)S(1)} %copy.21), channel_id=1, source_target_pairs={{1,0},{2,1},{3,2},{4,3},{5,4},{6,5},{7,6},{0,7},{9,8},{10,9},{11,1... | collective-permute-start | bytes 36872 | tf_op jit(solution)/shard_map/ppermute | solution.py:24
  152.8 5.9 collective-permute-start.2
  160.4 6.8 %copy-start.8 = (bf16[1,2,3,1024,256]{4,3,2,1,0:T(8,128)(2,1)S(1)}, bf16[1,2,3,1024,256]{4,3,2,1,0:T(8,128)(2,1)}, u32[]{:S(2)}) copy-start(bf16[1,2,3,1024,256]{4,3,2,1,0:T(8,128)(2,1)} %param.9) | copy-start | bytes 9437188
  160.4 6.8 %copy-start.56 = (f32[3,1024,256]{2,1,0:T(8,128)S(1)}, f32[3,1024,256]{2,1,0:T(8,128)}, u32[]{:S(2)}) copy-start(f32[3,1024,256]{2,1,0:T(8,128)} %fusion.18) | copy-start | bytes 9437188
  174.1 4.7 copy-start.74
  174.1 10.1 %copy-start.86 = (s32[1,1024]{1,0:T(1,128)S(1)}, s32[1,1024]{1,0:T(1,128)}, u32[]{:S(2)}) copy-start(s32[1,1024]{1,0:T(1,128)} %param.12) | copy-start | bytes 12292
  178.8 18.0 %copy-start.85 = (f32[1,1024]{1,0:T(1,128)S(1)}, f32[1,1024]{1,0:T(1,128)}, u32[]{:S(2)}) copy-start(f32[1,1024]{1,0:T(1,128)} %param.8) | copy-start | bytes 12292
  178.8 18.0 %copy-start.84 = (f32[1,1024]{1,0:T(1,128)S(1)}, f32[1,1024]{1,0:T(1,128)}, u32[]{:S(2)}) copy-start(f32[1,1024]{1,0:T(1,128)} %param.11) | copy-start | bytes 12292
  178.8 71.6 %collective-permute-start.9 = (f32[3,1024,256]{2,1,0:T(8,128)}, f32[3,1024,256]{2,1,0:T(8,128)}, u32[]{:S(2)}, u32[]{:S(2)}) collective-permute-start(f32[3,1024,256]{2,1,0:T(8,128)} %get-tuple-element.105), channel_id=1, source_target_pairs={{0,8},{8,16},{16,24},{1,9},{9,17},{17,25},{2,10},{10,18},{18,26},{... | collective-permute-start | bytes 9437192 | tf_op jit(solution)/shard_map/ppermute | solution.py:13
  215.9 8.5 %collective-permute-start.3 = (f32[3,1024,1]{1,2,0:T(1,128)S(1)}, f32[3,1024,1]{1,2,0:T(1,128)S(1)}, u32[]{:S(2)}, u32[]{:S(2)}) collective-permute-start(f32[3,1024,1]{1,2,0:T(1,128)S(1)} %copy.25), channel_id=1, source_target_pairs={{1,0},{2,1},{3,2},{4,3},{5,4},{6,5},{7,6},{0,7},{9,8},{10,9},{11,1... | collective-permute-start | bytes 36872 | tf_op jit(solution)/shard_map/ppermute | solution.py:24
  220.1 6.0 collective-permute-start.4
  227.8 6.6 copy-start.57
  227.8 6.6 copy-start.67
  227.8 6.6 copy-start.69
  227.8 6.6 copy-start.71
  235.1 6.4 copy-start.39
  235.1 6.4 copy-start.41
  235.1 6.4 copy-start.43
  238.4 12.0 %copy-start.16 = (f32[3,1024,256]{2,1,0:T(8,128)S(1)}, f32[3,1024,256]{2,1,0:T(8,128)}, u32[]{:S(2)}) copy-start(f32[3,1024,256]{2,1,0:T(8,128)} %get-tuple-element.27) | copy-start | bytes 9437188
  287.8 7.8 %copy-start.17 = (f32[3,1024,256]{2,1,0:T(8,128)S(1)}, f32[3,1024,256]{2,1,0:T(8,128)}, u32[]{:S(2)}) copy-start(f32[3,1024,256]{2,1,0:T(8,128)} %get-tuple-element.27) | copy-start | bytes 9437188
  351.0 71.5 %collective-permute-start.15 = (f32[3,1024,256]{2,1,0:T(8,128)}, f32[3,1024,256]{2,1,0:T(8,128)}, u32[]{:S(2)}, u32[]{:S(2)}) collective-permute-start(f32[3,1024,256]{2,1,0:T(8,128)} %get-tuple-element.17), channel_id=1, source_target_pairs={{8,0},{16,8},{24,16},{9,1},{17,9},{25,17},{10,2},{18,10},{26,18},{... | collective-permute-start | bytes 9437192 | tf_op jit(solution)/shard_map/ppermute | solution.py:13
  356.2 3.0 collective-permute-start.10
  359.2 4.0 collective-permute-start.11
  364.9 8.1 %copy-start.1 = (f32[3,1024,256]{2,1,0:T(8,128)S(1)}, f32[3,1024,256]{2,1,0:T(8,128)}, u32[]{:S(2)}) copy-start(f32[3,1024,256]{2,1,0:T(8,128)} %copy-done) | copy-start | bytes 9437188
  364.9 8.1 %copy-start.9 = (bf16[1,2,3,1024,256]{4,3,2,1,0:T(8,128)(2,1)S(1)}, bf16[1,2,3,1024,256]{4,3,2,1,0:T(8,128)(2,1)}, u32[]{:S(2)}) copy-start(bf16[1,2,3,1024,256]{4,3,2,1,0:T(8,128)(2,1)} %param.9) | copy-start | bytes 9437188
  380.0 8.0 %collective-permute-start.12 = (f32[3,1024,1]{1,2,0:T(1,128)S(1)}, f32[3,1024,1]{1,2,0:T(1,128)S(1)}, u32[]{:S(2)}, u32[]{:S(2)}) collective-permute-start(f32[3,1024,1]{1,2,0:T(1,128)S(1)} %copy.41), channel_id=1, source_target_pairs={{1,0},{2,1},{3,2},{4,3},{5,4},{6,5},{7,6},{0,7},{9,8},{10,9},{11,1... | collective-permute-start | bytes 36872 | tf_op jit(solution)/shard_map/ppermute | solution.py:24
  382.2 7.5 %collective-permute-start.13 = (f32[3,1024,1]{1,2,0:T(1,128)S(1)}, f32[3,1024,1]{1,2,0:T(1,128)S(1)}, u32[]{:S(2)}, u32[]{:S(2)}) collective-permute-start(f32[3,1024,1]{1,2,0:T(1,128)S(1)} %copy.43), channel_id=1, source_target_pairs={{0,1},{1,2},{2,3},{3,4},{4,5},{5,6},{6,7},{7,0},{8,9},{9,10},{10,1... | collective-permute-start | bytes 36872 | tf_op jit(solution)/shard_map/ppermute | solution.py:23
  391.4 6.7 copy-start.10
  391.4 6.7 copy-start.29
  391.4 6.7 copy-start.50
  391.4 6.7 copy-start.52
  432.1 6.6 collective-permute-start.16
  434.0 6.4 collective-permute-start.17
  442.0 6.7 copy-start.11
  442.0 6.7 copy-start.58
  458.1 71.8 %collective-permute-start.14 = (f32[3,1024,256]{2,1,0:T(8,128)}, f32[3,1024,256]{2,1,0:T(8,128)}, u32[]{:S(2)}, u32[]{:S(2)}) collective-permute-start(f32[3,1024,256]{2,1,0:T(8,128)} %pad_maximum_fusion.46), channel_id=1, source_target_pairs={{0,8},{8,16},{16,24},{1,9},{9,17},{17,25},{2,10},{10,18},{18,26},{... | collective-permute-start | bytes 9437192 | tf_op jit(solution)/shard_map/ppermute | solution.py:13
  507.6 8.0 %collective-permute-start.18 = (f32[3,1024,1]{1,2,0:T(1,128)S(1)}, f32[3,1024,1]{1,2,0:T(1,128)S(1)}, u32[]{:S(2)}, u32[]{:S(2)}) collective-permute-start(f32[3,1024,1]{1,2,0:T(1,128)S(1)} %copy.49), channel_id=1, source_target_pairs={{1,0},{2,1},{3,2},{4,3},{5,4},{6,5},{7,6},{0,7},{9,8},{10,9},{11,1... | collective-permute-start | bytes 36872 | tf_op jit(solution)/shard_map/ppermute | solution.py:24
  511.3 6.0 collective-permute-start.19
  519.0 6.6 copy-start.55
  519.0 6.7 copy-start.61
  519.0 6.7 copy-start.63
  519.0 6.7 copy-start.65
  569.9 5.5 copy-start.13
  569.9 5.5 copy-start.21
  569.9 5.6 copy-start.25
  606.4 10.0 %copy-start.18 = (f32[3,1024,256]{2,1,0:T(8,128)S(1)}, f32[3,1024,256]{2,1,0:T(8,128)}, u32[]{:S(2)}) copy-start(f32[3,1024,256]{2,1,0:T(8,128)} %get-tuple-element.23) | copy-start | bytes 9437188
  606.4 10.0 %copy-start.22 = (f32[3,1024,256]{2,1,0:T(8,128)S(1)}, f32[3,1024,256]{2,1,0:T(8,128)}, u32[]{:S(2)}) copy-start(f32[3,1024,256]{2,1,0:T(8,128)} %get-tuple-element.74) | copy-start | bytes 9437188
  663.4 7.1 %copy-start.5 = (f32[1,3,1024,256]{3,2,1,0:T(8,128)S(1)}, f32[1,3,1024,256]{3,2,1,0:T(8,128)}, u32[]{:S(2)}) copy-start(f32[1,3,1024,256]{3,2,1,0:T(8,128)} %get-tuple-element.29) | copy-start | bytes 9437188
  663.4 7.1 %copy-start.40 = (f32[1,1024,256]{2,1,0:T(8,128)S(1)}, f32[1,1024,256]{2,1,0:T(8,128)}, u32[]{:S(2)}) copy-start(f32[1,1024,256]{2,1,0:T(8,128)} %copy-done.39) | copy-start | bytes 3145732
  663.4 7.0 %copy-start.42 = (f32[1,1024,256]{2,1,0:T(8,128)S(1)}, f32[1,1024,256]{2,1,0:T(8,128)}, u32[]{:S(2)}) copy-start(f32[1,1024,256]{2,1,0:T(8,128)} %copy-done.41) | copy-start | bytes 3145732
  663.4 7.0 %copy-start.44 = (f32[1,1024,256]{2,1,0:T(8,128)S(1)}, f32[1,1024,256]{2,1,0:T(8,128)}, u32[]{:S(2)}) copy-start(f32[1,1024,256]{2,1,0:T(8,128)} %copy-done.43) | copy-start | bytes 3145732
  663.5 7.0 %copy-start.59 = (f32[1,3,1024,256]{3,2,1,0:T(8,128)S(1)}, f32[1,3,1024,256]{3,2,1,0:T(8,128)}, u32[]{:S(2)}) copy-start(f32[1,3,1024,256]{3,2,1,0:T(8,128)} %reshape.522) | copy-start | bytes 9437188
  (43 other events, 123.2 us)
